TPU v7x, 128 devices: a whole 4x4x4 slice. The times are simulated.
128 devices in a mesh: pipe: 2 (over x_hi), tensor: 4 (over z), dp: 16 (over x_lo, y, core).
Axes of the slice: x: 4 (x_hi: 2, x_lo: 2; x = x_hi * 2 + x_lo), y: 4, z: 4, core: 2. Of those that a mesh axis runs over, the one named last changes fastest.
Arguments:
- tokens: bfloat16 [8192, 1024], P('dp', 'tensor'), may hold values from -6 to 6
- lengths: int32 [64, 4], P('dp'), may hold values from 1 to 85, 128 in all within a row
- ln_gain: bfloat16 [2, 2, 1024], P('pipe'), may hold values from 0.099609375 to 1.8984375
- ln_bias: bfloat16 [2, 2, 1024], P('pipe'), may hold values from -3 to 3
- joined_weight: bfloat16 [2, 1024, 3, 1024], P('pipe', None, None, 'tensor'), may hold values from -0.1875 to 0.1875
- joined_bias: bfloat16 [2, 3, 1024], P('pipe', None, 'tensor'), may hold values from -3 to 3
- dense_weight: bfloat16 [2, 1024, 1024], P('pipe', 'tensor'), may hold values from -0.5 to 0.5
- up_weight: bfloat16 [2, 1024, 4096], P('pipe', None, 'tensor'), may hold values from -0.1875 to 0.1875
- up_bias: bfloat16 [2, 4096], P('pipe', 'tensor'), may hold values from -3 to 3
- down_weight: bfloat16 [2, 4096, 1024], P('pipe', 'tensor'), may hold values from -0.09375 to 0.09375
- output_bias: bfloat16 [2, 2, 1024], P('pipe'), may hold values from -3 to 3
- cotangent: bfloat16 [8192, 1024], P('dp', 'tensor'), may hold values from -6 to 6
Outputs:
- section_out: bfloat16 [2, 8192, 1024], P('pipe', 'dp', 'tensor')
- input_grad: bfloat16 [2, 8192, 1024], P('pipe', 'dp', 'tensor')
- grad_ln_gain: float32 [2, 2, 1024], P('pipe')
- grad_ln_bias: float32 [2, 2, 1024], P('pipe')
- grad_joined: float32 [2, 1024, 3, 1024], P('pipe', None, None, 'tensor')
- grad_joined_bias: float32 [2, 3, 1024], P('pipe', None, 'tensor')
- grad_dense: float32 [2, 1024, 1024], P('pipe', 'tensor')
- grad_up: float32 [2, 1024, 4096], P('pipe', None, 'tensor')
- grad_up_bias: float32 [2, 4096], P('pipe', 'tensor')
- grad_down: float32 [2, 4096, 1024], P('pipe', 'tensor')
- grad_output_bias: float32 [2, 2, 1024], P('pipe')
Inputs may be any that keep to these rules, and one draw needn't show every extreme that they name: Row b gives, in order, the lengths of the 4 sequences that fill block b (tokens b * 128 to (b + 1) * 128 - 1); every row sums to 128.
All inputs are finite; a program needn't handle non-finite values.
Results may differ from a plain program's by a relative error of at most 0.035.
Values may be sent and summed in bfloat16 or wider, within the bound.
No kernel may reach another device: no remote copies, remote signals or barrier semaphores. Data moves between devices by JAX's collectives and lax.ppermute only.
A program may use at most 192 MiB of HBM per device.

v0:
```python
import jax
import jax.numpy as jnp
from jax import lax
from jax.sharding import PartitionSpec as P

HD = 64
ROT = 16
MB = 128
NMB = 4
EPSILON = 1e-05
MASKED = -1e30


def passed_along(x, axis, by):
    peers = lax.axis_size(axis)
    pairs = [(i, i + by) for i in range(peers) if 0 <= i + by < peers]
    return lax.ppermute(x, axis, pairs)


def as_sent(x):
    return jax.tree.map(lambda a: a.astype(jnp.bfloat16) if a.dtype == jnp.float32 else a, x)


def positions(lengths, block_rows):
    seq_count = lengths.shape[1]
    counter = jnp.arange(seq_count, dtype=jnp.int32)
    lower_tri = (counter[:, None] >= counter[None, :]).astype(jnp.int32)
    seg_ends = jnp.sum(lengths[:, None, :] * lower_tri[None, :, :], axis=2)
    starts = seg_ends - lengths
    row_index = jnp.arange(block_rows, dtype=jnp.int32)
    segment = jnp.sum((row_index[None, :, None] >= seg_ends[:, None, :]).astype(jnp.int32), axis=2)
    member = (segment[:, :, None] == counter[None, None, :]).astype(jnp.int32)
    place = row_index[None, :] - jnp.sum(member * starts[:, None, :], axis=2)
    return (segment, place)


def rotary(place):
    half_rot = ROT // 2
    inv_freq = jnp.power(10000.0, -2.0 * jnp.arange(half_rot, dtype=jnp.float32) / ROT)
    angles = place.astype(jnp.float32)[..., None] * inv_freq
    return (jnp.cos(angles), jnp.sin(angles))


def rotate(heads_in, cosv, sinv):
    half_rot = ROT // 2
    first_half = heads_in[..., :half_rot]
    second_half = heads_in[..., half_rot:ROT]
    cos_rows = cosv[:, None, :]
    sin_rows = sinv[:, None, :]
    return jnp.concatenate(
        [
            first_half * cos_rows - second_half * sin_rows,
            second_half * cos_rows + first_half * sin_rows,
            heads_in[..., ROT:],
        ],
        axis=-1,
    )


def rotate_back(heads_in, cosv, sinv):
    half_rot = ROT // 2
    first_half = heads_in[..., :half_rot]
    second_half = heads_in[..., half_rot:ROT]
    cos_rows = cosv[:, None, :]
    sin_rows = sinv[:, None, :]
    return jnp.concatenate(
        [
            first_half * cos_rows + second_half * sin_rows,
            second_half * cos_rows - first_half * sin_rows,
            heads_in[..., ROT:],
        ],
        axis=-1,
    )


def exact_gelu(values):
    return jax.nn.gelu(values, approximate=False)


def allowed_keys(segment):
    row_index = jnp.arange(segment.shape[0], dtype=jnp.int32)
    return (segment[:, None] == segment[None, :]) & (row_index[None, :] <= row_index[:, None])


def contract_rows(left, right):
    return lax.dot_general(
        left, right, (((0,), (0,)), ((), ())), preferred_element_type=jnp.float32
    )


def contract_cols(left, right):
    return lax.dot_general(
        left, right, (((1,), (1,)), ((), ())), preferred_element_type=jnp.float32
    )


def per_device(
    tokens,
    lengths,
    ln_gain,
    ln_bias,
    joined_weight,
    joined_bias,
    dense_weight,
    up_weight,
    up_bias,
    down_weight,
    output_bias,
    cotangent,
):
    leading = lax.axis_index("pipe") == 0
    model_width = joined_weight.shape[1]
    local_width = joined_weight.shape[3]
    local_heads = local_width // HD
    hidden_local = up_weight.shape[2]
    quarter = tokens.shape[1]
    score_scale = HD ** (-0.5)
    ln_gains = ln_gain[0].astype(jnp.float32)
    ln_shifts = ln_bias[0].astype(jnp.float32)
    joined_mat = joined_weight[0].reshape(model_width, 3 * local_width)
    joined_add = joined_bias[0].astype(jnp.float32).reshape(3 * local_width)
    dense_mat = dense_weight[0]
    up_mat = up_weight[0]
    up_add = up_bias[0].astype(jnp.float32)
    down_mat = down_weight[0]
    bias_sum = output_bias[0, 0].astype(jnp.float32) + output_bias[0, 1].astype(jnp.float32)
    input_rows, output_grads = (
        lax.all_gather(tokens, "tensor", axis=1, tiled=True),
        lax.all_gather(cotangent, "tensor", axis=1, tiled=True),
    )
    segment_all, place_all = positions(lengths, MB)
    cos_all, sin_all = rotary(place_all)

    def pick(early_val, late_val):
        return jax.tree.map(
            lambda upper_val, lower_val: jnp.where(leading, upper_val, lower_val),
            early_val,
            late_val,
        )

    received = jnp.zeros((MB, model_width), jnp.bfloat16)
    tick_outputs = []
    tick_stored = []
    for section_tick in range(NMB + 1):
        early_block = min(section_tick, NMB - 1)
        late_block = max(section_tick - 1, 0)
        block_rows = jnp.where(
            leading, input_rows[early_block * MB : (early_block + 1) * MB], received
        )
        segment, cosv, sinv = pick(
            (segment_all[early_block], cos_all[early_block], sin_all[early_block]),
            (segment_all[late_block], cos_all[late_block], sin_all[late_block]),
        )
        inputs = block_rows.astype(jnp.float32)
        row_mean = jnp.mean(inputs, axis=1, keepdims=True)
        centred = inputs - row_mean
        forward_inv_scale = lax.rsqrt(jnp.mean(centred * centred, axis=1, keepdims=True) + EPSILON)
        forward_normed = centred * forward_inv_scale
        forward_h_attn = (forward_normed * ln_gains[0] + ln_shifts[0]).astype(jnp.bfloat16)
        forward_h_mlp = (forward_normed * ln_gains[1] + ln_shifts[1]).astype(jnp.bfloat16)
        joined_proj = (
            jnp.dot(forward_h_attn, joined_mat, preferred_element_type=jnp.float32) + joined_add
        )
        forward_block_len = block_rows.shape[0]
        forward_queries = rotate(
            joined_proj[:, :local_width].reshape(forward_block_len, local_heads, HD), cosv, sinv
        ).astype(jnp.bfloat16)
        forward_keys_rot = rotate(
            joined_proj[:, local_width : 2 * local_width].reshape(
                forward_block_len, local_heads, HD
            ),
            cosv,
            sinv,
        ).astype(jnp.bfloat16)
        forward_values = (
            joined_proj[:, 2 * local_width :]
            .reshape(forward_block_len, local_heads, HD)
            .astype(jnp.bfloat16)
        )
        forward_scores = (
            jnp.einsum(
                "qhd,khd->hqk",
                forward_queries,
                forward_keys_rot,
                preferred_element_type=jnp.float32,
            )
            * score_scale
        )
        forward_scores = jnp.where(allowed_keys(segment)[None], forward_scores, MASKED)
        row_top = jnp.max(forward_scores, axis=2, keepdims=True)
        exponent = jnp.exp(forward_scores - row_top)
        row_total = jnp.sum(exponent, axis=2, keepdims=True)
        forward_log_total = row_top + jnp.log(row_total)
        weights_low = (exponent / row_total).astype(jnp.bfloat16)
        forward_context = jnp.einsum(
            "hqk,khd->qhd", weights_low, forward_values, preferred_element_type=jnp.float32
        )
        forward_context = forward_context.reshape(forward_block_len, local_width).astype(
            jnp.bfloat16
        )
        forward_up_proj = (
            jnp.dot(forward_h_mlp, up_mat, preferred_element_type=jnp.float32) + up_add
        )
        forward_activated = exact_gelu(forward_up_proj).astype(jnp.bfloat16)
        partial_value = jnp.dot(forward_context, dense_mat, preferred_element_type=jnp.float32)
        partial_value = partial_value + jnp.dot(
            forward_activated, down_mat, preferred_element_type=jnp.float32
        )
        branches = lax.psum(partial_value.astype(jnp.bfloat16), "tensor").astype(jnp.float32)
        result = inputs + branches + bias_sum
        forward_stored = (
            forward_normed,
            forward_inv_scale,
            forward_h_attn,
            forward_h_mlp,
            forward_queries,
            forward_keys_rot,
            forward_values,
            forward_log_total,
            forward_context,
            forward_up_proj,
            forward_activated,
        )
        result, stored = (result, forward_stored)
        result_low = result.astype(jnp.bfloat16)
        tick_outputs.append(result_low)
        tick_stored.append((stored, segment, cosv, sinv))
        if section_tick < NMB:
            received = passed_along(result_low, "pipe", 1)
    column_start = lax.axis_index("tensor") * quarter
    section_rows = jnp.concatenate(
        [jnp.where(leading, tick_outputs[block], tick_outputs[block + 1]) for block in range(NMB)],
        axis=0,
    )
    section_out = lax.dynamic_slice_in_dim(section_rows, column_start, quarter, 1)[None]
    returned = jnp.zeros((MB, model_width), jnp.bfloat16)
    tick_grads = []
    totals = None
    for section_tick in range(NMB + 1):
        own_block = min(section_tick, NMB - 1)
        late_tick = max(section_tick - 1, 0)
        upper_tick = min(section_tick + 1, NMB)
        from_output = output_grads[own_block * MB : (own_block + 1) * MB]
        if section_tick == NMB:
            from_output = jnp.zeros_like(from_output)
        grad_rows = jnp.where(leading, returned, from_output)
        stored, segment, cosv, sinv = pick(tick_stored[late_tick], tick_stored[upper_tick])
        (
            normed,
            inv_scale,
            h_attn,
            h_mlp,
            queries,
            keys_rot,
            values,
            log_total,
            context,
            up_proj,
            activated,
        ) = stored
        block_len = grad_rows.shape[0]
        grad_wide = grad_rows.astype(jnp.float32)
        column_sum = jnp.sum(grad_wide, axis=0)
        backward_grad_dense = contract_rows(context, grad_rows)
        backward_grad_down = contract_rows(activated, grad_rows)
        d_context = contract_cols(grad_rows, dense_mat).astype(jnp.bfloat16)
        d_act = contract_cols(grad_rows, down_mat)
        unused, slope_back = jax.vjp(exact_gelu, up_proj)
        d_up = slope_back(d_act)[0].astype(jnp.bfloat16)
        grad_up_add = jnp.sum(d_up.astype(jnp.float32), axis=0)
        backward_grad_up = contract_rows(h_mlp, d_up)
        d_hmlp = contract_cols(d_up, up_mat)
        scores = (
            jnp.einsum("qhd,khd->hqk", queries, keys_rot, preferred_element_type=jnp.float32)
            * score_scale
        )
        scores = jnp.where(allowed_keys(segment)[None], scores, MASKED)
        weights_soft = jnp.exp(scores - log_total)
        d_context3 = d_context.reshape(block_len, local_heads, HD)
        d_values = jnp.einsum(
            "hqk,qhd->khd",
            weights_soft.astype(jnp.bfloat16),
            d_context3,
            preferred_element_type=jnp.float32,
        ).astype(jnp.bfloat16)
        d_weights = jnp.einsum(
            "qhd,khd->hqk", d_context3, values, preferred_element_type=jnp.float32
        )
        row_delta = jnp.sum(weights_soft * d_weights, axis=2, keepdims=True)
        d_scores = (weights_soft * (d_weights - row_delta)).astype(jnp.bfloat16)
        d_queries = (
            jnp.einsum("hqk,khd->qhd", d_scores, keys_rot, preferred_element_type=jnp.float32)
            * score_scale
        )
        d_keys = (
            jnp.einsum("hqk,qhd->khd", d_scores, queries, preferred_element_type=jnp.float32)
            * score_scale
        )
        d_queries = (
            rotate_back(d_queries, cosv, sinv).reshape(block_len, local_width).astype(jnp.bfloat16)
        )
        d_keys = (
            rotate_back(d_keys, cosv, sinv).reshape(block_len, local_width).astype(jnp.bfloat16)
        )
        d_joined = jnp.concatenate(
            [d_queries, d_keys, d_values.reshape(block_len, local_width)], axis=1
        )
        grad_joined_add = jnp.sum(d_joined.astype(jnp.float32), axis=0)
        backward_grad_joined = contract_rows(h_attn, d_joined)
        d_hattn = contract_cols(d_joined, joined_mat)
        d_hattn, d_hmlp = (
            lax.psum(d_hattn.astype(jnp.bfloat16), "tensor").astype(jnp.float32),
            lax.psum(d_hmlp.astype(jnp.bfloat16), "tensor").astype(jnp.float32),
        )
        grad_gains = jnp.concatenate(
            [jnp.sum(d_hattn * normed, axis=0), jnp.sum(d_hmlp * normed, axis=0)]
        )
        grad_shifts = jnp.concatenate([jnp.sum(d_hattn, axis=0), jnp.sum(d_hmlp, axis=0)])
        d_norm = d_hattn * ln_gains[0] + d_hmlp * ln_gains[1]
        grad_input = grad_wide + inv_scale * (
            d_norm
            - jnp.mean(d_norm, axis=1, keepdims=True)
            - normed * jnp.mean(d_norm * normed, axis=1, keepdims=True)
        )
        small_terms = jnp.concatenate(
            [grad_gains, grad_shifts, column_sum, column_sum, grad_joined_add, grad_up_add]
        )
        terms = (
            backward_grad_joined[None],
            backward_grad_dense[None],
            backward_grad_up[None],
            backward_grad_down[None],
            small_terms[None],
        )
        grad_input, terms = (grad_input, terms)
        grad_low = grad_input.astype(jnp.bfloat16)
        tick_grads.append(grad_low)
        if totals is None:
            totals = terms
        else:
            totals = jax.tree.map(lambda older, newer: older + newer, totals, terms)
        if section_tick < NMB:
            returned = passed_along(grad_low, "pipe", -1)
    totals = jax.tree.map(
        lambda part: part.astype(jnp.float32),
        lax.psum_scatter(as_sent(totals), "dp", scatter_dimension=1, tiled=True),
    )
    summed = jax.tree.map(
        lambda part, own: part.astype(own.dtype),
        lax.all_gather(as_sent(totals), "dp", axis=1, tiled=True),
        totals,
    )
    grad_rows_all = jnp.concatenate(
        [jnp.where(leading, tick_grads[block + 1], tick_grads[block]) for block in range(NMB)],
        axis=0,
    )
    input_grad = lax.dynamic_slice_in_dim(grad_rows_all, column_start, quarter, 1)[None]
    grad_joined = summed[0].reshape(1, model_width, 3, local_width)
    grad_dense = summed[1]
    grad_up = summed[2]
    grad_down = summed[3]
    small_sum = summed[4][0]
    offset = 0
    grad_ln_gain = small_sum[offset : offset + 2 * model_width].reshape(1, 2, model_width)
    offset = offset + 2 * model_width
    grad_ln_bias = small_sum[offset : offset + 2 * model_width].reshape(1, 2, model_width)
    offset = offset + 2 * model_width
    grad_output_bias = small_sum[offset : offset + 2 * model_width].reshape(1, 2, model_width)
    offset = offset + 2 * model_width
    grad_joined_bias = small_sum[offset : offset + 3 * local_width].reshape(1, 3, local_width)
    offset = offset + 3 * local_width
    grad_up_bias = small_sum[offset : offset + hidden_local].reshape(1, hidden_local)
    return (
        section_out,
        input_grad,
        grad_ln_gain,
        grad_ln_bias,
        grad_joined,
        grad_joined_bias,
        grad_dense,
        grad_up,
        grad_up_bias,
        grad_down,
        grad_output_bias,
    )


def solution(mesh):
    placed = (
        P("dp", "tensor"),
        P("dp", None),
        P("pipe", None, None),
        P("pipe", None, None),
        P("pipe", None, None, "tensor"),
        P("pipe", None, "tensor"),
        P("pipe", "tensor", None),
        P("pipe", None, "tensor"),
        P("pipe", "tensor"),
        P("pipe", "tensor", None),
        P("pipe", None, None),
        P("dp", "tensor"),
    )
    return jax.shard_map(
        per_device,
        mesh=mesh,
        in_specs=placed,
        out_specs=(
            P("pipe", "dp", "tensor"),
            P("pipe", "dp", "tensor"),
            P("pipe", None, None),
            P("pipe", None, None),
            P("pipe", None, None, "tensor"),
            P("pipe", None, "tensor"),
            P("pipe", "tensor", None),
            P("pipe", None, "tensor"),
            P("pipe", "tensor"),
            P("pipe", "tensor", None),
            P("pipe", None, None),
        ),
        check_vma=False,
    )
```

profile of v0, /device:TPU:1, one launch (start us, length us, event | category | flops | bytes accessed | tf_op | source)
XLA Modules:
  0.0 983.1 jit_solution(12664540825030383722)
XLA Ops:
  17.0 21.2 %all-gather.6.cloned.1.call-done = bf16[512,1024]{1,0:T(8,128)(2,1)} async-done(((bf16[512,256]{1,0:T(8,128)(2,1)}), bf16[512,1024]{1,0:T(8,128)(2,1)}) %all-gather.6.cloned.1.call-update) | async-done | bytes 1048592 | tf_op jit(solution)/shard_map/all_gather | solution.py:128
  60.0 32.3 %all-reduce.13.cloned.1.call-done = bf16[128,1024]{1,0:T(8,128)(2,1)} async-done(((bf16[128,1024]{1,0:T(8,128)(2,1)}), bf16[128,1024]{1,0:T(8,128)(2,1)}) %all-reduce.13.cloned.1.call-update) | async-done | bytes 262160 | tf_op jit(solution)/shard_map/psum | solution.py:209
  93.4 5.1 collective-permute-start
  99.2 22.5 %all-gather.8.cloned.1.call-done = bf16[512,1024]{1,0:T(8,128)(2,1)} async-done(((bf16[512,256]{1,0:T(8,128)(2,1)}), bf16[512,1024]{1,0:T(8,128)(2,1)}) %all-gather.8.cloned.1.call-update) | async-done | bytes 1048592 | tf_op jit(solution)/shard_map/all_gather | solution.py:129
  137.5 3.6 convert_reduce_fusion.24
  149.2 42.2 %all-reduce.23.cloned.1.call-done = (bf16[128,1024]{1,0:T(8,128)(2,1)}, bf16[128,1024]{1,0:T(8,128)(2,1)}, bf16[128,1024]{1,0:T(8,128)(2,1)}) async-done(((bf16[128,1024]{1,0:T(8,128)(2,1)}, bf16[128,1024]{1,0:T(8,128)(2,1)}, bf16[128,1024]{1,0:T(8,128)(2,1)}), (bf16[128,1024]{1,0:T(8,128)(2,1)}, bf16[128,1024]{1,0:T(8,128)(2,1)}, bf16[128,1024]{1,0:T(8,128)(2,1)})) %all-reduce.23.cloned.1.call-update) | async-done | bytes 786448 | tf_op jit(solution)/shard_map/psum | solution.py:313
  193.4 4.7 collective-permute-start.1
  198.0 3.9 fusion.386
  242.2 5.4 fusion.377
  247.6 38.0 %all-reduce.21.cloned.1.call-done = (bf16[128,1024]{1,0:T(8,128)(2,1)}, bf16[128,1024]{1,0:T(8,128)(2,1)}, bf16[128,1024]{1,0:T(8,128)(2,1)}) async-done(((bf16[128,1024]{1,0:T(8,128)(2,1)}, bf16[128,1024]{1,0:T(8,128)(2,1)}, bf16[128,1024]{1,0:T(8,128)(2,1)}), (bf16[128,1024]{1,0:T(8,128)(2,1)}, bf16[128,1024]{1,0:T(8,128)(2,1)}, bf16[128,1024]{1,0:T(8,128)(2,1)})) %all-reduce.21.cloned.1.call-update) | async-done | bytes 786448 | tf_op jit(solution)/shard_map/psum | solution.py:313
  287.6 4.5 collective-permute-start.2
  341.1 6.1 fusion.375
  347.2 37.1 %all-reduce.19.cloned.1.call-done = (bf16[128,1024]{1,0:T(8,128)(2,1)}, bf16[128,1024]{1,0:T(8,128)(2,1)}, bf16[128,1024]{1,0:T(8,128)(2,1)}) async-done(((bf16[128,1024]{1,0:T(8,128)(2,1)}, bf16[128,1024]{1,0:T(8,128)(2,1)}, bf16[128,1024]{1,0:T(8,128)(2,1)}), (bf16[128,1024]{1,0:T(8,128)(2,1)}, bf16[128,1024]{1,0:T(8,128)(2,1)}, bf16[128,1024]{1,0:T(8,128)(2,1)})) %all-reduce.19.cloned.1.call-update) | async-done | bytes 786448 | tf_op jit(solution)/shard_map/psum | solution.py:313
  389.2 4.7 collective-permute-start.3
  401.4 3.9 collective-permute-done.6
  435.3 37.3 %all-reduce.17.cloned.1.call-done = (bf16[128,1024]{1,0:T(8,128)(2,1)}, bf16[128,1024]{1,0:T(8,128)(2,1)}) async-done(((bf16[128,1024]{1,0:T(8,128)(2,1)}, bf16[128,1024]{1,0:T(8,128)(2,1)}), (bf16[128,1024]{1,0:T(8,128)(2,1)}, bf16[128,1024]{1,0:T(8,128)(2,1)})) %all-reduce.17.cloned.1.call-update) | async-done | bytes 524304 | tf_op jit(solution)/shard_map/psum | solution.py:313
  481.0 4.9 collective-permute-done.7
  500.8 5.3 fusion.42
  506.4 4.1 fusion.384
  517.6 4.2 fusion
  554.3 53.3 %reduce-scatter.8.cloned.1.call-done = bf16[1,64,768]{2,1,0:T(8,128)(2,1)} async-done(((bf16[1,1024,768]{2,1,0:T(8,128)(2,1)}), bf16[1,64,768]{2,1,0:T(8,128)(2,1)}) %reduce-scatter.8.cloned.1.call-update) | async-done | bytes 98320 | tf_op jit(solution)/shard_map/reduce_scatter | solution.py:346
  607.7 64.2 %reduce-scatter.14.cloned.1.call-done = bf16[1,64,1024]{2,1,0:T(8,128)(2,1)} async-done(((bf16[1,1024,1024]{2,1,0:T(8,128)(2,1)}), bf16[1,64,1024]{2,1,0:T(8,128)(2,1)}) %reduce-scatter.14.cloned.1.call-update) | async-done | bytes 131088 | tf_op jit(solution)/shard_map/reduce_scatter | solution.py:346
  672.0 64.7 %reduce-scatter.12.cloned.1.call-done = bf16[1,64,1024]{2,1,0:T(8,128)(2,1)} async-done(((bf16[1,1024,1024]{2,1,0:T(8,128)(2,1)}), bf16[1,64,1024]{2,1,0:T(8,128)(2,1)}) %reduce-scatter.12.cloned.1.call-update) | async-done | bytes 131088 | tf_op jit(solution)/shard_map/reduce_scatter | solution.py:346
  740.6 60.6 %reduce-scatter.16.cloned.1.call-done = bf16[496,1]{1,0:T(8,128)(2,1)} async-done(((bf16[7936,1]{1,0:T(8,128)(2,1)}), bf16[496,1]{1,0:T(8,128)(2,1)}) %reduce-scatter.16.cloned.1.call-update) | async-done | bytes 1008
  802.5 53.0 %all-reduce = bf16[7936]{0:T(1024)(128)(2,1)S(1)} all-reduce(bf16[7936]{0:T(1024)(128)(2,1)S(1)} %dynamic-update-slice), channel_id=1, replica_groups=mesh['pipe'=2,'tensor'=4,'dp'=16] {'dp'}, use_global_device_ids=true, to_apply=%add | all-reduce | flops 7936 | bytes 31744
  858.7 4.6 reduce-scatter.10.cloned.1.call-done
  863.3 22.4 %all_gather.25 = bf16[1,256,1024]{2,1,0:T(8,128)(2,1)S(1)} all-gather(bf16[1,16,1024]{2,1,0:T(8,128)(2,1)} %reduce-scatter.10.cloned.1.call-done), channel_id=1, replica_groups=mesh['pipe'=2,'tensor'=4,'dp'=16] {'dp'}, dimensions={1}, use_global_device_ids=true | all-gather | bytes 557056 | tf_op jit(solution)/shard_map/all_gather | solution.py:350
  886.8 14.1 %all-gather.10.cloned.1.call-done = bf16[1,1024,768]{2,1,0:T(8,128)(2,1)} async-done(((bf16[1,64,768]{2,1,0:T(8,128)(2,1)}), bf16[1,1024,768]{2,1,0:T(8,128)(2,1)}) %all-gather.10.cloned.1.call-update) | async-done | bytes 1572880 | tf_op jit(solution)/shard_map/all_gather | solution.py:350
  907.5 29.0 %all-gather.14.cloned.1.call-done = bf16[1,1024,1024]{2,1,0:T(8,128)(2,1)} async-done(((bf16[1,64,1024]{2,1,0:T(8,128)(2,1)}), bf16[1,1024,1024]{2,1,0:T(8,128)(2,1)}) %all-gather.14.cloned.1.call-update) | async-done | bytes 2097168 | tf_op jit(solution)/shard_map/all_gather | solution.py:350
  936.6 4.1 convert_element_type.728
  940.6 31.6 %all-gather.12.cloned.1.call-done = bf16[1,1024,1024]{2,1,0:T(8,128)(2,1)} async-done(((bf16[1,64,1024]{2,1,0:T(8,128)(2,1)}), bf16[1,1024,1024]{2,1,0:T(8,128)(2,1)}) %all-gather.12.cloned.1.call-update) | async-done | bytes 2097168 | tf_op jit(solution)/shard_map/all_gather | solution.py:350
  972.2 4.1 convert_element_type.725
  (1057 shorter events, 266.6 us)
Async XLA Ops:
  7.2 31.0 %all-gather.6.cloned.1.call-start = ((), (), s32[]{:S(2)}) async-start(), calls=%async_computation.5 | async-start | bytes 1310720 | tf_op jit(solution)/shard_map/all_gather | solution.py:128
  7.9 84.3 %all-reduce.13.cloned.1.call-start = ((), (), s32[]{:S(2)}) async-start(), calls=%async_computation.6 | async-start | bytes 524288 | tf_op jit(solution)/shard_map/psum | solution.py:209
  50.6 71.1 %all-gather.8.cloned.1.call-start = ((), (), s32[]{:S(2)}) async-start(), calls=%async_computation.7 | async-start | bytes 1310720 | tf_op jit(solution)/shard_map/all_gather | solution.py:129
  51.3 140.1 %all-reduce.23.cloned.1.call-start = ((), (), s32[]{:S(2)}) async-start(), calls=%async_computation.20 | async-start | bytes 1572864 | tf_op jit(solution)/shard_map/psum | solution.py:313
  93.4 29.7 %collective-permute-start = (bf16[128,1024]{1,0:T(8,128)(2,1)S(1)}, bf16[128,1024]{1,0:T(8,128)(2,1)S(1)}, u32[]{:S(2)}, u32[]{:S(2)}) collective-permute-start(bf16[128,1024]{1,0:T(8,128)(2,1)S(1)} %fusion.193), channel_id=1, source_target_pairs={{0,64},{1,65},{2,66},{3,67},{4,68},{5,69},{6,70},{7,71},{8,72},{9,... | collective-permute-start | bytes 786440 | tf_op jit(solution)/shard_map/ppermute | solution.py:17
  146.4 139.2 %all-reduce.21.cloned.1.call-start = ((), (), s32[]{:S(2)}) async-start(), calls=%async_computation.19 | async-start | bytes 1572864 | tf_op jit(solution)/shard_map/psum | solution.py:313
  193.4 8.6 collective-permute-start.1
  214.9 9.0 collective-permute-start.4
  237.8 146.5 %all-reduce.19.cloned.1.call-start = ((), (), s32[]{:S(2)}) async-start(), calls=%async_computation.18 | async-start | bytes 1572864 | tf_op jit(solution)/shard_map/psum | solution.py:313
  287.6 7.8 collective-permute-start.2
  312.5 8.9 collective-permute-start.5
  336.9 92.9 %copy-start.70 = (bf16[128,4,64]{0,2,1:T(8,128)(2,1)}, bf16[128,4,64]{0,2,1:T(8,128)(2,1)S(1)}, u32[]{:S(2)}) copy-start(bf16[128,4,64]{0,2,1:T(8,128)(2,1)S(1)} %pad_maximum_fusion.19) | copy-start | bytes 196612
  338.1 134.5 %all-reduce.17.cloned.1.call-start = ((), (), s32[]{:S(2)}) async-start(), calls=%async_computation.17 | async-start | bytes 1048576 | tf_op jit(solution)/shard_map/psum | solution.py:313
  389.2 9.2 collective-permute-start.3
  396.5 8.7 collective-permute-start.6
  429.8 117.8 %all-reduce.15.cloned.1.call-start = ((), (), s32[]{:S(2)}) async-start(), calls=%async_computation.16 | async-start | bytes 1572864 | tf_op jit(solution)/shard_map/psum | solution.py:313
  477.2 8.8 collective-permute-start.7
  498.7 108.9 %reduce-scatter.8.cloned.1.call-start = ((), (), s32[]{:S(2)}) async-start(), calls=%async_computation.8 | async-start | bytes 1671168 | tf_op jit(solution)/shard_map/reduce_scatter | solution.py:346
  506.1 165.8 %reduce-scatter.14.cloned.1.call-start = ((), (), s32[]{:S(2)}) async-start(), calls=%async_computation.13 | async-start | bytes 2228224 | tf_op jit(solution)/shard_map/reduce_scatter | solution.py:346
  521.9 214.7 %reduce-scatter.12.cloned.1.call-start = ((), (), s32[]{:S(2)}) async-start(), calls=%async_computation.11 | async-start | bytes 2228224 | tf_op jit(solution)/shard_map/reduce_scatter | solution.py:346
  545.3 256.0 %reduce-scatter.16.cloned.1.call-start = ((), (), s32[]{:S(2)}) async-start(), calls=%async_computation.15 | async-start | bytes 2158592
  551.2 312.2 %reduce-scatter.10.cloned.1.call-start = ((), (), s32[]{:S(2)}) async-start(), calls=%async_computation.10 | async-start | bytes 557056 | tf_op jit(solution)/shard_map/reduce_scatter | solution.py:346
  551.2 185.4 %copy-start.343 = (u32[128]{0:T(128)S(1)}, u32[128]{0:T(128)}, u32[]{:S(2)}) copy-start(u32[128]{0:T(128)} %constant.134) | copy-start | bytes 1540
  551.2 186.8 %copy-start.48 = (bf16[128,1024]{1,0:T(8,128)(2,1)S(1)}, bf16[128,1024]{1,0:T(8,128)(2,1)}, u32[]{:S(2)}) copy-start(bf16[128,1024]{1,0:T(8,128)(2,1)} %copy-done.47) | copy-start | bytes 786436
  551.2 186.8 %copy-start.121 = (f32[1,1,1024]{2,1,0:T(1,128)S(1)}, f32[1,1,1024]{2,1,0:T(1,128)}, u32[]{:S(2)}) copy-start(f32[1,1,1024]{2,1,0:T(1,128)} %copy-done.119) | copy-start | bytes 12292
  551.3 186.8 %copy-start.151 = (f32[128]{0:T(128)S(1)}, f32[128]{0:T(128)}, u32[]{:S(2)}) copy-start(f32[128]{0:T(128)} %copy-done.148) | copy-start | bytes 1540
  551.3 186.8 %copy-start.164 = (f32[128]{0:T(128)S(1)}, f32[128]{0:T(128)}, u32[]{:S(2)}) copy-start(f32[128]{0:T(128)} %copy-done.158) | copy-start | bytes 1540
  551.3 186.8 %copy-start.322 = (f32[128]{0:T(128)S(1)}, f32[128]{0:T(128)}, u32[]{:S(2)}) copy-start(f32[128]{0:T(128)} %get-tuple-element.276) | copy-start | bytes 1540
  554.3 185.5 %copy-start.62 = (bf16[128,1024]{1,0:T(8,128)(2,1)S(1)}, bf16[128,1024]{1,0:T(8,128)(2,1)}, u32[]{:S(2)}) copy-start(bf16[128,1024]{1,0:T(8,128)(2,1)} %get-tuple-element.144) | copy-start | bytes 786436
  554.3 346.6 %all-gather.10.cloned.1.call-start = ((), (), s32[]{:S(2)}) async-start(), calls=%async_computation.9 | async-start | bytes 1671168 | tf_op jit(solution)/shard_map/all_gather | solution.py:350
  607.6 328.9 %all-gather.14.cloned.1.call-start = ((), (), s32[]{:S(2)}) async-start(), calls=%async_computation.14 | async-start | bytes 2228224 | tf_op jit(solution)/shard_map/all_gather | solution.py:350
  671.9 300.3 %all-gather.12.cloned.1.call-start = ((), (), s32[]{:S(2)}) async-start(), calls=%async_computation.12 | async-start | bytes 2228224 | tf_op jit(solution)/shard_map/all_gather | solution.py:350
  (342 other events, 2877.5 us)
Sparse Core Ops, SparseCore 0:
  9.7 28.4 all-gather.5
  50.7 41.4 all-reduce.12
  94.0 27.6 all-gather.7
  146.5 44.8 all-reduce.22
  237.9 47.6 all-reduce.20
  338.2 46.0 all-reduce.18
  429.9 42.7 all-reduce.16
  498.8 45.1 all-reduce.14
  546.6 60.9 reduce-scatter.7
  609.8 61.9 reduce-scatter.13
  674.8 61.7 reduce-scatter.11
  739.5 61.7 reduce-scatter.15
  804.2 59.0 reduce-scatter.9
  865.0 35.9 all-gather.9
  902.6 33.9 all-gather.13
  938.2 33.9 all-gather.11
where the time goes:
time: 990 us; the launch traced here: 983 us
  waiting for transfers between devices  568 us (57%)
  matrix products  146 us (15%)
  blocking collectives  75.5 us (8%)
  other arithmetic  75.3 us (8%)
  local copies, waits for them, and re-layouts  71.9 us (7%)
  starting transfers between devices  26.5 us (3%)
  between operations  19.7 us (2%)
    reduce_scatter x4, waiting for transfers between devices, per_device(): lax.psum_scatter(as_sent(totals), 'dp', scatter_dimension=1, tiled=True)  187 us
    psum x5, waiting for transfers between devices, per_device(): lax.psum(d_hmlp.astype(jnp.bfloat16), 'tensor').astype(jnp.float32)  155 us
    all_gather x3, waiting for transfers between devices, per_device(): lax.all_gather(as_sent(totals), 'dp', axis=1, tiled=True)  74.7 us
    unnamed x17, waiting for transfers between devices  62.2 us
    dot_general x20, matrix products, contract_rows(): lax.dot_general(left, right, (((0,), (0,)), ((), ())), preferred_element_...  59.5 us
    unnamed x1, blocking collectives  53 us
    unnamed x742, local copies, waits for them, and re-layouts  32.7 us
    psum x1, waiting for transfers between devices, per_device(): lax.psum(partial_value.astype(jnp.bfloat16), 'tensor').astype(jnp.float32)  32.3 us
  transfers between devices with their start and end apart: 24, of which 19 were waited for; matrix products, arithmetic and copies ran while one was open for 14% of the time, Pallas kernels for 0%

commit v1 on v0

--- a/solution.py
+++ b/solution.py
@@ -310,7 +310,9 @@
         d_hattn = contract_cols(d_joined, joined_mat)
         d_hattn, d_hmlp = (
             lax.psum(d_hattn.astype(jnp.bfloat16), "tensor").astype(jnp.float32),
-            lax.psum(d_hmlp.astype(jnp.bfloat16), "tensor").astype(jnp.float32),
+            jnp.sum(lax.all_gather(d_hmlp.astype(jnp.bfloat16), "tensor"), axis=0).astype(
+                jnp.float32
+            ),
         )
         grad_gains = jnp.concatenate(
             [jnp.sum(d_hattn * normed, axis=0), jnp.sum(d_hmlp * normed, axis=0)]

time: 990 us -> 1090 us (1.10)
  waiting for transfers between devices: 568 us -> 660 us
  other arithmetic: 75.3 us -> 89.1 us
  local copies, waits for them, and re-layouts: 71.9 us -> 59.7 us
    reduce_scatter x4, waiting for transfers between devices: 187 us -> 250 us  [per_device(): lax.psum_scatter(as_sent(totals), 'dp', scatter_dimension=1, tiled=True)]
    all_gather x0 -> x5, waiting for transfers between devices: none -> 57 us  [per_device(): lax.all_gather(d_hmlp.astype(jnp.bfloat16), 'tensor')]
    all_gather x3, waiting for transfers between devices: 74.7 us -> 40.6 us  [per_device(): lax.all_gather(as_sent(totals), 'dp', axis=1, tiled=True)]
    psum x5, waiting for transfers between devices: 155 us -> 182 us  [per_device(): lax.psum(d_hattn.astype(jnp.bfloat16), 'tensor').astype(jnp.float32)]
    unnamed x17 -> x22, waiting for transfers between devices: 62.2 us -> 40.6 us
    unnamed x742 -> x712, local copies, waits for them, and re-layouts: 32.7 us -> 19.8 us
    dot_general x20, matrix products: 59.5 us -> 48.3 us  [contract_rows(): lax.dot_general(left, right, (((0,), (0,)), ((), ())), preferred_element_...]
  transfers between devices with their start and end apart: 24 -> 29, of which waited for: 19 -> 23; matrix products, arithmetic and copies ran while one was open for 14% -> 15% of each run, Pallas kernels for 0% -> 0%
where the time goes in v1:
time: 1090 us; the launch traced here: 1070 us
  waiting for transfers between devices  660 us (61%)
  matrix products  142 us (13%)
  other arithmetic  89.1 us (8%)
  blocking collectives  75.4 us (7%)
  local copies, waits for them, and re-layouts  59.7 us (5%)
  starting transfers between devices  27.8 us (3%)
  between operations  19.9 us (2%)
    reduce_scatter x4, waiting for transfers between devices, per_device(): lax.psum_scatter(as_sent(totals), 'dp', scatter_dimension=1, tiled=True)  250 us
    psum x5, waiting for transfers between devices, per_device(): lax.psum(d_hattn.astype(jnp.bfloat16), 'tensor').astype(jnp.float32)  182 us
    all_gather x5, waiting for transfers between devices, per_device(): lax.all_gather(d_hmlp.astype(jnp.bfloat16), 'tensor')  57 us
    unnamed x1, blocking collectives  53 us
    dot_general x20, matrix products, contract_rows(): lax.dot_general(left, right, (((0,), (0,)), ((), ())), preferred_element_...  48.3 us
    unnamed x22, waiting for transfers between devices  40.6 us
    all_gather x3, waiting for transfers between devices, per_device(): lax.all_gather(as_sent(totals), 'dp', axis=1, tiled=True)  40.6 us
    dot_general x20, matrix products, contract_cols(): lax.dot_general(left, right, (((1,), (1,)), ((), ())), preferred_element_...  34.8 us
  transfers between devices with their start and end apart: 29, of which 23 were waited for; matrix products, arithmetic and copies ran while one was open for 15% of the time, Pallas kernels for 0%

profile of v1, /device:TPU:1, one launch (start us, length us, event | category | flops | bytes accessed | tf_op | source)
XLA Modules:
  0.0 1073.7 jit_solution(8525296251708746101)
XLA Ops:
  16.4 21.8 %all-gather.16.cloned.1.call-done = bf16[512,1024]{1,0:T(8,128)(2,1)} async-done(((bf16[512,256]{1,0:T(8,128)(2,1)}), bf16[512,1024]{1,0:T(8,128)(2,1)}) %all-gather.16.cloned.1.call-update) | async-done | bytes 1048592 | tf_op jit(solution)/shard_map/all_gather | solution.py:128
  56.9 34.3 %all-reduce.12.cloned.1.call-done = bf16[128,1024]{1,0:T(8,128)(2,1)} async-done(((bf16[128,1024]{1,0:T(8,128)(2,1)}), bf16[128,1024]{1,0:T(8,128)(2,1)}) %all-reduce.12.cloned.1.call-update) | async-done | bytes 262160 | tf_op jit(solution)/shard_map/psum | solution.py:209
  92.4 4.6 collective-permute-start
  98.4 22.3 %all-gather.18.cloned.1.call-done = bf16[512,1024]{1,0:T(8,128)(2,1)} async-done(((bf16[512,256]{1,0:T(8,128)(2,1)}), bf16[512,1024]{1,0:T(8,128)(2,1)}) %all-gather.18.cloned.1.call-update) | async-done | bytes 1048592 | tf_op jit(solution)/shard_map/all_gather | solution.py:129
  145.1 35.9 %all-reduce.22.cloned.1.call-done = (bf16[128,1024]{1,0:T(8,128)(2,1)}, bf16[128,1024]{1,0:T(8,128)(2,1)}) async-done(((bf16[128,1024]{1,0:T(8,128)(2,1)}, bf16[128,1024]{1,0:T(8,128)(2,1)}), (bf16[128,1024]{1,0:T(8,128)(2,1)}, bf16[128,1024]{1,0:T(8,128)(2,1)})) %all-reduce.22.cloned.1.call-update) | async-done | bytes 524304 | tf_op jit(solution)/shard_map/psum | solution.py:312
  182.8 5.2 collective-permute-start.1
  190.7 18.1 %all-gather.26.cloned.1.call-done = bf16[512,1024]{1,0:T(8,128)(2,1)} async-done(((bf16[128,1024]{1,0:T(8,128)(2,1)}), bf16[512,1024]{1,0:T(8,128)(2,1)}) %all-gather.26.cloned.1.call-update) | async-done | bytes 1048592 | tf_op jit(solution)/shard_map/all_gather | solution.py:313
  257.5 33.9 %all-reduce.20.cloned.1.call-done = (bf16[128,1024]{1,0:T(8,128)(2,1)}, bf16[128,1024]{1,0:T(8,128)(2,1)}) async-done(((bf16[128,1024]{1,0:T(8,128)(2,1)}, bf16[128,1024]{1,0:T(8,128)(2,1)}), (bf16[128,1024]{1,0:T(8,128)(2,1)}, bf16[128,1024]{1,0:T(8,128)(2,1)})) %all-reduce.20.cloned.1.call-update) | async-done | bytes 524304 | tf_op jit(solution)/shard_map/psum | solution.py:312
  293.3 5.4 collective-permute-start.2
  298.7 6.1 fusion.377
  304.8 14.1 %all-gather.28.cloned.1.call-done = bf16[512,1024]{1,0:T(8,128)(2,1)} async-done(((bf16[128,1024]{1,0:T(8,128)(2,1)}), bf16[512,1024]{1,0:T(8,128)(2,1)}) %all-gather.28.cloned.1.call-update) | async-done | bytes 1048592 | tf_op jit(solution)/shard_map/all_gather | solution.py:313
  373.0 11.6 %all-gather.30.cloned.1.call-done = bf16[512,1024]{1,0:T(8,128)(2,1)} async-done(((bf16[128,1024]{1,0:T(8,128)(2,1)}), bf16[512,1024]{1,0:T(8,128)(2,1)}) %all-gather.30.cloned.1.call-update) | async-done | bytes 1048592 | tf_op jit(solution)/shard_map/all_gather | solution.py:313
  386.0 43.8 %all-reduce.18.cloned.1.call-done = (bf16[128,1024]{1,0:T(8,128)(2,1)}, bf16[128,1024]{1,0:T(8,128)(2,1)}) async-done(((bf16[128,1024]{1,0:T(8,128)(2,1)}, bf16[128,1024]{1,0:T(8,128)(2,1)}), (bf16[128,1024]{1,0:T(8,128)(2,1)}, bf16[128,1024]{1,0:T(8,128)(2,1)})) %all-reduce.18.cloned.1.call-update) | async-done | bytes 524304 | tf_op jit(solution)/shard_map/psum | solution.py:312
  434.5 4.9 collective-permute-start.3
  484.0 13.2 %all-gather.32.cloned.1.call-done = bf16[512,1024]{1,0:T(8,128)(2,1)} async-done(((bf16[128,1024]{1,0:T(8,128)(2,1)}), bf16[512,1024]{1,0:T(8,128)(2,1)}) %all-gather.32.cloned.1.call-update) | async-done | bytes 1048592 | tf_op jit(solution)/shard_map/all_gather | solution.py:313
  499.4 41.4 %all-reduce.14.cloned.1.call-done = bf16[128,1024]{1,0:T(8,128)(2,1)} async-done(((bf16[128,1024]{1,0:T(8,128)(2,1)}), bf16[128,1024]{1,0:T(8,128)(2,1)}) %all-reduce.14.cloned.1.call-update) | async-done | bytes 262160 | tf_op jit(solution)/shard_map/psum | solution.py:312
  549.1 4.8 collective-permute-done.7
  568.9 6.8 fusion.42
  576.1 4.1 fusion.375
  586.0 4.2 fusion
  606.4 27.2 %all-reduce.16.cloned.1.call-done = (bf16[128,1024]{1,0:T(8,128)(2,1)}, bf16[128,1024]{1,0:T(8,128)(2,1)}) async-done(((bf16[128,1024]{1,0:T(8,128)(2,1)}, bf16[128,1024]{1,0:T(8,128)(2,1)}), (bf16[128,1024]{1,0:T(8,128)(2,1)}, bf16[128,1024]{1,0:T(8,128)(2,1)})) %all-reduce.16.cloned.1.call-update) | async-done | bytes 524304 | tf_op jit(solution)/shard_map/psum | solution.py:312
  637.7 59.3 %reduce-scatter.8.cloned.1.call-done = bf16[1,64,768]{2,1,0:T(8,128)(2,1)} async-done(((bf16[1,1024,768]{2,1,0:T(8,128)(2,1)}), bf16[1,64,768]{2,1,0:T(8,128)(2,1)}) %reduce-scatter.8.cloned.1.call-update) | async-done | bytes 98320 | tf_op jit(solution)/shard_map/reduce_scatter | solution.py:348
  697.1 64.6 %reduce-scatter.14.cloned.1.call-done = bf16[1,64,1024]{2,1,0:T(8,128)(2,1)} async-done(((bf16[1,1024,1024]{2,1,0:T(8,128)(2,1)}), bf16[1,64,1024]{2,1,0:T(8,128)(2,1)}) %reduce-scatter.14.cloned.1.call-update) | async-done | bytes 131088 | tf_op jit(solution)/shard_map/reduce_scatter | solution.py:348
  761.7 64.8 %reduce-scatter.12.cloned.1.call-done = bf16[1,64,1024]{2,1,0:T(8,128)(2,1)} async-done(((bf16[1,1024,1024]{2,1,0:T(8,128)(2,1)}), bf16[1,64,1024]{2,1,0:T(8,128)(2,1)}) %reduce-scatter.12.cloned.1.call-update) | async-done | bytes 131088 | tf_op jit(solution)/shard_map/reduce_scatter | solution.py:348
  827.8 61.0 %reduce-scatter.10.cloned.1.call-done = bf16[1,16,1024]{2,1,0:T(8,128)(2,1)} async-done(((bf16[1,256,1024]{2,1,0:T(8,128)(2,1)}), bf16[1,16,1024]{2,1,0:T(8,128)(2,1)}) %reduce-scatter.10.cloned.1.call-update) | async-done | bytes 32784 | tf_op jit(solution)/shard_map/reduce_scatter | solution.py:348
  888.8 22.4 %all_gather.65 = bf16[1,256,1024]{2,1,0:T(8,128)(2,1)S(1)} all-gather(bf16[1,16,1024]{2,1,0:T(8,128)(2,1)} %reduce-scatter.10.cloned.1.call-done), channel_id=1, replica_groups=mesh['pipe'=2,'tensor'=4,'dp'=16] {'dp'}, dimensions={1}, use_global_device_ids=true | all-gather | bytes 557056 | tf_op jit(solution)/shard_map/all_gather | solution.py:352
  914.8 38.9 %reduce-scatter.16.cloned.1.call-done = bf16[496,1]{1,0:T(8,128)(2,1)} async-done(((bf16[7936,1]{1,0:T(8,128)(2,1)}), bf16[496,1]{1,0:T(8,128)(2,1)}) %reduce-scatter.16.cloned.1.call-update) | async-done | bytes 1008
  955.0 53.0 %all-reduce = bf16[7936]{0:T(1024)(128)(2,1)S(1)} all-reduce(bf16[7936]{0:T(1024)(128)(2,1)S(1)} %dynamic-update-slice), channel_id=1, replica_groups=mesh['pipe'=2,'tensor'=4,'dp'=16] {'dp'}, use_global_device_ids=true, to_apply=%add | all-reduce | flops 7936 | bytes 31744
  1017.8 9.1 all-gather.24.cloned.1.call-done
  1026.9 4.2 convert_element_type.738
  1031.1 31.5 %all-gather.22.cloned.1.call-done = bf16[1,1024,1024]{2,1,0:T(8,128)(2,1)} async-done(((bf16[1,64,1024]{2,1,0:T(8,128)(2,1)}), bf16[1,1024,1024]{2,1,0:T(8,128)(2,1)}) %all-gather.22.cloned.1.call-update) | async-done | bytes 2097168 | tf_op jit(solution)/shard_map/all_gather | solution.py:352
  1062.5 4.1 convert_element_type.735
  (1047 shorter events, 277.1 us)
Async XLA Ops:
  7.2 31.0 %all-gather.16.cloned.1.call-start = ((), (), s32[]{:S(2)}) async-start(), calls=%async_computation.5 | async-start | bytes 1310720 | tf_op jit(solution)/shard_map/all_gather | solution.py:128
  7.9 83.3 %all-reduce.12.cloned.1.call-start = ((), (), s32[]{:S(2)}) async-start(), calls=%async_computation.6 | async-start | bytes 524288 | tf_op jit(solution)/shard_map/psum | solution.py:209
  49.6 71.1 %all-gather.18.cloned.1.call-start = ((), (), s32[]{:S(2)}) async-start(), calls=%async_computation.7 | async-start | bytes 1310720 | tf_op jit(solution)/shard_map/all_gather | solution.py:129
  50.3 130.7 %all-reduce.22.cloned.1.call-start = ((), (), s32[]{:S(2)}) async-start(), calls=%async_computation.25 | async-start | bytes 1048576 | tf_op jit(solution)/shard_map/psum | solution.py:312
  92.4 29.7 %collective-permute-start = (bf16[128,1024]{1,0:T(8,128)(2,1)S(1)}, bf16[128,1024]{1,0:T(8,128)(2,1)S(1)}, u32[]{:S(2)}, u32[]{:S(2)}) collective-permute-start(bf16[128,1024]{1,0:T(8,128)(2,1)S(1)} %fusion.193), channel_id=1, source_target_pairs={{0,64},{1,65},{2,66},{3,67},{4,68},{5,69},{6,70},{7,71},{8,72},{9,... | collective-permute-start | bytes 786440 | tf_op jit(solution)/shard_map/ppermute | solution.py:17
  137.8 71.1 %all-gather.26.cloned.1.call-start = ((), (), s32[]{:S(2)}) async-start(), calls=%async_computation.16 | async-start | bytes 1310720 | tf_op jit(solution)/shard_map/all_gather | solution.py:313
  143.2 148.2 %all-reduce.20.cloned.1.call-start = ((), (), s32[]{:S(2)}) async-start(), calls=%async_computation.24 | async-start | bytes 1048576 | tf_op jit(solution)/shard_map/psum | solution.py:312
  182.8 27.5 %collective-permute-start.1 = (bf16[128,1024]{1,0:T(8,128)(2,1)S(1)}, bf16[128,1024]{1,0:T(8,128)(2,1)}, u32[]{:S(2)}, u32[]{:S(2)}) collective-permute-start(bf16[128,1024]{1,0:T(8,128)(2,1)S(1)} %get-tuple-element.139), channel_id=1, source_target_pairs={{0,64},{1,65},{2,66},{3,67},{4,68},{5,69},{6,70},{7,71},{8,72},{9,... | collective-permute-start | bytes 786440 | tf_op jit(solution)/shard_map/ppermute | solution.py:17
  229.1 9.9 collective-permute-start.4
  249.3 69.6 %all-gather.28.cloned.1.call-start = ((), (), s32[]{:S(2)}) async-start(), calls=%async_computation.17 | async-start | bytes 1310720 | tf_op jit(solution)/shard_map/all_gather | solution.py:313
  255.4 129.2 %all-gather.30.cloned.1.call-start = ((), (), s32[]{:S(2)}) async-start(), calls=%async_computation.18 | async-start | bytes 1310720 | tf_op jit(solution)/shard_map/all_gather | solution.py:313
  293.3 27.8 %collective-permute-start.2 = (bf16[128,1024]{1,0:T(8,128)(2,1)S(1)}, bf16[128,1024]{1,0:T(8,128)(2,1)}, u32[]{:S(2)}, u32[]{:S(2)}) collective-permute-start(bf16[128,1024]{1,0:T(8,128)(2,1)S(1)} %get-tuple-element.134), channel_id=1, source_target_pairs={{0,64},{1,65},{2,66},{3,67},{4,68},{5,69},{6,70},{7,71},{8,72},{9,... | collective-permute-start | bytes 786440 | tf_op jit(solution)/shard_map/ppermute | solution.py:17
  339.2 10.2 collective-permute-start.5
  358.8 71.0 %all-reduce.18.cloned.1.call-start = ((), (), s32[]{:S(2)}) async-start(), calls=%async_computation.23 | async-start | bytes 1048576 | tf_op jit(solution)/shard_map/psum | solution.py:312
  365.8 131.4 %all-gather.32.cloned.1.call-start = ((), (), s32[]{:S(2)}) async-start(), calls=%async_computation.19 | async-start | bytes 1310720 | tf_op jit(solution)/shard_map/all_gather | solution.py:313
  434.5 8.8 collective-permute-start.3
  441.8 8.7 collective-permute-start.6
  471.8 68.9 %all-reduce.14.cloned.1.call-start = ((), (), s32[]{:S(2)}) async-start(), calls=%async_computation.8 | async-start | bytes 524288 | tf_op jit(solution)/shard_map/psum | solution.py:312
  480.1 124.8 %all-gather.34.cloned.1.call-start = ((), (), s32[]{:S(2)}) async-start(), calls=%async_computation.20 | async-start | bytes 1310720 | tf_op jit(solution)/shard_map/all_gather | solution.py:313
  545.2 8.7 collective-permute-start.7
  563.0 70.6 %all-reduce.16.cloned.1.call-start = ((), (), s32[]{:S(2)}) async-start(), calls=%async_computation.22 | async-start | bytes 1048576 | tf_op jit(solution)/shard_map/psum | solution.py:312
  568.9 128.1 %reduce-scatter.8.cloned.1.call-start = ((), (), s32[]{:S(2)}) async-start(), calls=%async_computation.9 | async-start | bytes 1671168 | tf_op jit(solution)/shard_map/reduce_scatter | solution.py:348
  575.8 185.8 %reduce-scatter.14.cloned.1.call-start = ((), (), s32[]{:S(2)}) async-start(), calls=%async_computation.14 | async-start | bytes 2228224 | tf_op jit(solution)/shard_map/reduce_scatter | solution.py:348
  590.3 236.1 %reduce-scatter.12.cloned.1.call-start = ((), (), s32[]{:S(2)}) async-start(), calls=%async_computation.12 | async-start | bytes 2228224 | tf_op jit(solution)/shard_map/reduce_scatter | solution.py:348
  599.5 289.2 %reduce-scatter.10.cloned.1.call-start = ((), (), s32[]{:S(2)}) async-start(), calls=%async_computation.11 | async-start | bytes 557056 | tf_op jit(solution)/shard_map/reduce_scatter | solution.py:348
  604.8 349.0 %reduce-scatter.16.cloned.1.call-start = ((), (), s32[]{:S(2)}) async-start(), calls=%async_computation.21 | async-start | bytes 2158592
  637.6 274.7 %copy-start.48 = (bf16[128,1024]{1,0:T(8,128)(2,1)S(1)}, bf16[128,1024]{1,0:T(8,128)(2,1)}, u32[]{:S(2)}) copy-start(bf16[128,1024]{1,0:T(8,128)(2,1)} %get-tuple-element.88) | copy-start | bytes 786436
  637.6 274.8 %copy-start.126 = (f32[1,1,1024]{2,1,0:T(1,128)S(1)}, f32[1,1,1024]{2,1,0:T(1,128)}, u32[]{:S(2)}) copy-start(f32[1,1,1024]{2,1,0:T(1,128)} %copy-done.124) | copy-start | bytes 12292
  637.6 274.8 %copy-start.312 = (f32[128]{0:T(128)S(1)}, f32[128]{0:T(128)}, u32[]{:S(2)}) copy-start(f32[128]{0:T(128)} %get-tuple-element.270) | copy-start | bytes 1540
  637.6 373.5 %all-gather.20.cloned.1.call-start = ((), (), s32[]{:S(2)}) async-start(), calls=%async_computation.10 | async-start | bytes 1671168 | tf_op jit(solution)/shard_map/all_gather | solution.py:352
  697.0 329.8 %all-gather.24.cloned.1.call-start = ((), (), s32[]{:S(2)}) async-start(), calls=%async_computation.15 | async-start | bytes 2228224 | tf_op jit(solution)/shard_map/all_gather | solution.py:352
  761.6 300.9 %all-gather.22.cloned.1.call-start = ((), (), s32[]{:S(2)}) async-start(), calls=%async_computation.13 | async-start | bytes 2228224 | tf_op jit(solution)/shard_map/all_gather | solution.py:352
  (332 other events, 4145.2 us)
Sparse Core Ops, SparseCore 0:
  9.7 28.4 all-gather.15
  49.7 41.4 all-reduce.11
  93.0 27.6 all-gather.17
  137.9 43.0 all-reduce.21
  183.2 25.6 all-gather.25
  249.5 41.9 all-reduce.19
  293.2 25.6 all-gather.27
  358.9 25.6 all-gather.29
  387.1 42.6 all-reduce.17
  471.9 25.1 all-gather.31
  499.6 41.0 all-reduce.13
  563.1 25.3 all-gather.33
  590.9 42.6 all-reduce.15
  635.8 61.1 reduce-scatter.7
  699.9 61.6 reduce-scatter.13
  764.6 61.8 reduce-scatter.11
  829.4 59.3 reduce-scatter.9
  891.6 62.1 reduce-scatter.15
  955.4 35.5 all-gather.19
  992.6 34.1 all-gather.23
  1028.6 33.9 all-gather.21
